TPU v7x, 32 devices: a whole 2x2x4 slice. The times are simulated.
32 devices in a mesh: grp: 8 (over y, x, core), blk: 4 (over z).
Axes of the slice: x: 2, y: 2, z: 4, core: 2. Of those that a mesh axis runs over, the one named last changes fastest.
Arguments:
- inputs: bfloat16 [8, 2, 1024, 640], P('grp', None, 'blk'), may hold values from -6 to 6
- cotangent: bfloat16 [8, 2, 1024, 640], P('grp', None, 'blk'), may hold values from -6 to 6
- master_attend: float32 [640, 1536], P('blk'), may hold values from -0.25 to 0.25
- master_merge: float32 [1024, 640], P('blk'), may hold values from -0.1875 to 0.1875
- master_expand: float32 [640, 4096], P('blk'), may hold values from -0.25 to 0.25
- master_reduce: float32 [2048, 640], P('blk'), may hold values from -0.125 to 0.125
- master_gains: float32 [3072], P('blk'), may hold values from -1 to 1
- moment_attend: float32 [640, 1536], P('blk'), may hold values from -3 to 3
- moment_merge: float32 [1024, 640], P('blk'), may hold values from -3 to 3
- moment_expand: float32 [640, 4096], P('blk'), may hold values from -3 to 3
- moment_reduce: float32 [2048, 640], P('blk'), may hold values from -3 to 3
- moment_gains: float32 [3072], P('blk'), may hold values from -3 to 3
- error_attend: float32 [8, 640, 1536], P('grp', 'blk'), may hold values from -192 to 192
- error_merge: float32 [8, 1024, 640], P('grp', 'blk'), may hold values from -192 to 192
- error_expand: float32 [8, 640, 4096], P('grp', 'blk'), may hold values from -192 to 192
- error_reduce: float32 [8, 2048, 640], P('grp', 'blk'), may hold values from -192 to 192
- start_attend: float32 [4, 1536, 8], P('blk'), may hold values from -6 to 6
- start_merge: float32 [4, 640, 8], P('blk'), may hold values from -6 to 6
- start_expand: float32 [4, 4096, 8], P('blk'), may hold values from -6 to 6
- start_reduce: float32 [4, 640, 8], P('blk'), may hold values from -6 to 6
Outputs:
- block_output: bfloat16 [8, 2, 1024, 640], P('grp', None, 'blk')
- input_grad: float32 [8, 2, 1024, 640], P('grp', None, 'blk')
- grad_attend: float32 [8, 640, 1536], P('grp', 'blk')
- grad_merge: float32 [8, 1024, 640], P('grp', 'blk')
- grad_expand: float32 [8, 640, 4096], P('grp', 'blk')
- grad_reduce: float32 [8, 2048, 640], P('grp', 'blk')
- grad_gains: float32 [8, 3072], P('grp', 'blk')
- left_attend: float32 [640, 8], P('blk')
- left_merge: float32 [1024, 8], P('blk')
- left_expand: float32 [640, 8], P('blk')
- left_reduce: float32 [2048, 8], P('blk')
- right_attend: float32 [4, 1536, 8], P('blk')
- right_merge: float32 [4, 640, 8], P('blk')
- right_expand: float32 [4, 4096, 8], P('blk')
- right_reduce: float32 [4, 640, 8], P('blk')
- residue_attend: float32 [8, 640, 1536], P('grp', 'blk')
- residue_merge: float32 [8, 1024, 640], P('grp', 'blk')
- residue_expand: float32 [8, 640, 4096], P('grp', 'blk')
- residue_reduce: float32 [8, 2048, 640], P('grp', 'blk')
- velocity_attend: float32 [640, 1536], P('blk')
- velocity_merge: float32 [1024, 640], P('blk')
- velocity_expand: float32 [640, 4096], P('blk')
- velocity_reduce: float32 [2048, 640], P('blk')
- velocity_gains: float32 [3072], P('blk')
- weight_attend: float32 [640, 1536], P('blk')
- weight_merge: float32 [1024, 640], P('blk')
- weight_expand: float32 [640, 4096], P('blk')
- weight_reduce: float32 [2048, 640], P('blk')
- weight_gains: float32 [3072], P('blk')
- copy_attend: bfloat16 [640, 1536], P('blk')
- copy_merge: bfloat16 [1024, 640], P('blk')
- copy_expand: bfloat16 [640, 4096], P('blk')
- copy_reduce: bfloat16 [2048, 640], P('blk')
- copy_gains: bfloat16 [3072], P('blk')
All inputs are finite; a program needn't handle non-finite values.
Results may differ from a plain program's by a relative error of at most 0.028.
Values may be sent and summed in bfloat16 or wider, within the bound.
No kernel may reach another device: no remote copies, remote signals or barrier semaphores. Data moves between devices by JAX's collectives and lax.ppermute only.
A program may use at most 192 MiB of HBM per device.

v0:
```python
import jax
import jax.numpy as jnp
from jax import lax
from jax.sharding import PartitionSpec as P

D = 640
NH = 4
HD = 256
FF = 2048
WINDOW = 512
SEG = 256
HQ = 1024
NORM_EPS = 1e-06
ROPE_BASE = 10000.0
ERROR_KEEP = 0.5
MOMENTUM = 0.9
STEP_RATE = 0.02
NEG_FILL = -1e30


def rmsnorm(values, gain_row):
    return (
        values
        * lax.rsqrt(jnp.mean(values * values, axis=-1, keepdims=True) + NORM_EPS)
        * (1.0 + gain_row)
    )


def rotate(values, cosine, sine_part):
    middle = values.shape[-1] // 2
    turned = jnp.concatenate([-values[..., middle:], values[..., :middle]], axis=-1)
    return values * cosine + turned * sine_part


def rope_tables(places):
    frequency = jnp.arange(HD // 2, dtype=jnp.float32)
    inverse = ROPE_BASE ** (-2.0 * frequency / HD)
    angles = places.astype(jnp.float32)[:, None] * inverse[None, :]
    angles = jnp.concatenate([angles, angles], axis=-1)
    return (jnp.cos(angles), jnp.sin(angles))


def prepare_heads(projected, gain_query, gain_key, cosine, sine_part):
    row_count = projected.shape[0]
    query_rows = projected[:, :HQ].reshape(row_count, NH, HD)
    keys_raw = projected[:, HQ : HQ + HD]
    values_raw = projected[:, HQ + HD :]
    query_rows = rotate(
        rmsnorm(query_rows, gain_query), cosine[:, None, :], sine_part[:, None, :]
    ) * HD ** (-0.5)
    keys_rot = rotate(rmsnorm(keys_raw, gain_key), cosine, sine_part)
    return (query_rows, keys_rot, values_raw)


def gated_gelu(gate_up):
    return jax.nn.gelu(gate_up[:, :FF], approximate=True) * gate_up[:, FF:]


def orthonormal(factor):
    columns = []
    for column in range(factor.shape[1]):
        vector = factor[:, column]
        for basis in columns:
            vector = vector - jnp.sum(basis * vector) * basis
        columns.append(vector * lax.rsqrt(jnp.sum(vector * vector) + NORM_EPS))
    return jnp.stack(columns, axis=1)


def contract_rows(left_side, right_side):
    return lax.dot_general(
        left_side, right_side, (((0,), (0,)), ((), ())), preferred_element_type=jnp.float32
    )


def contract_cols(left_side, right_side):
    return lax.dot_general(
        left_side, right_side, (((1,), (1,)), ((), ())), preferred_element_type=jnp.float32
    )


def on_device(
    inputs,
    cotangent,
    master_attend,
    master_merge,
    master_expand,
    master_reduce,
    master_gains,
    moment_attend,
    moment_merge,
    moment_expand,
    moment_reduce,
    moment_gains,
    error_attend,
    error_merge,
    error_expand,
    error_reduce,
    start_attend,
    start_merge,
    start_expand,
    start_reduce,
):
    blocks = lax.axis_size("blk")
    groups = lax.axis_size("grp")
    block_index = lax.axis_index("blk")
    prompt_size = SEG * blocks
    full_attend, full_merge, full_expand, full_reduce, gain_copy = (
        lax.all_gather(master_attend.astype(jnp.bfloat16), "blk", axis=0, tiled=True),
        lax.all_gather(master_merge.astype(jnp.bfloat16), "blk", axis=0, tiled=True),
        lax.all_gather(master_expand.astype(jnp.bfloat16), "blk", axis=0, tiled=True),
        lax.all_gather(master_reduce.astype(jnp.bfloat16), "blk", axis=0, tiled=True),
        lax.all_gather(master_gains.astype(jnp.bfloat16), "blk", axis=0, tiled=True),
    )
    gain_all = gain_copy.astype(jnp.float32)
    gain_first = gain_all[:D]
    gain_second = gain_all[D : 2 * D]
    gain_third = gain_all[2 * D : 3 * D]
    gain_fourth = gain_all[3 * D : 4 * D]
    gain_query = gain_all[4 * D : 4 * D + HD]
    gain_key = gain_all[4 * D + HD :]
    offsets = jnp.arange(SEG, dtype=jnp.int32)
    prompt_place = block_index * SEG + offsets
    reply_place = prompt_size + offsets
    cosine, sine_part = rope_tables(jnp.concatenate([prompt_place, reply_place]))
    rows_in = inputs[0].reshape(2 * SEG, D).astype(jnp.float32)
    normed_low = rmsnorm(rows_in, gain_first).astype(jnp.bfloat16)
    projected = jnp.dot(normed_low, full_attend, preferred_element_type=jnp.float32)
    query_rows, keys_rot, values_raw = prepare_heads(
        projected, gain_query, gain_key, cosine, sine_part
    )
    query_reduced = query_rows.astype(jnp.bfloat16).reshape(2, SEG, NH, HD)
    pair_low = jnp.concatenate([keys_rot, values_raw], axis=-1).astype(jnp.bfloat16)
    prompt_pairs = lax.all_gather(pair_low[:SEG], "blk", axis=0, tiled=True)
    padded = jnp.concatenate([jnp.zeros((WINDOW, 2 * HD), jnp.bfloat16), prompt_pairs], axis=0)
    window_pairs = lax.dynamic_slice_in_dim(padded, block_index * SEG, WINDOW + SEG, 0)
    reply_pairs = jnp.concatenate([prompt_pairs[prompt_size - WINDOW :], pair_low[SEG:]], axis=0)
    key_sets = jnp.stack([window_pairs, reply_pairs])
    key_reduced = key_sets[..., :HD]
    value_reduced = key_sets[..., HD:]
    span = jnp.arange(WINDOW + SEG, dtype=jnp.int32)
    key_place = jnp.stack(
        [
            block_index * SEG - WINDOW + span,
            jnp.where(span < WINDOW, prompt_size - WINDOW + span, prompt_size + span - WINDOW),
        ]
    )
    query_place = jnp.stack([prompt_place, reply_place])
    distance = query_place[:, :, None] - key_place[:, None, :]
    allowed = (key_place[:, None, :] >= 0) & (distance >= 0) & (distance < WINDOW)

    def score_block():
        products = jnp.einsum(
            "itge,iue->igtu", query_reduced, key_reduced, preferred_element_type=jnp.float32
        )
        return jnp.where(allowed[:, None], products, NEG_FILL)

    attention_scores = score_block()
    top_score = jnp.max(attention_scores, axis=-1, keepdims=True)
    log_total = top_score + jnp.log(
        jnp.sum(jnp.exp(attention_scores - top_score), axis=-1, keepdims=True)
    )
    probability_reduced = jnp.exp(attention_scores - log_total).astype(jnp.bfloat16)
    attended = jnp.einsum(
        "ayco,aox->acyx", probability_reduced, value_reduced, preferred_element_type=jnp.float32
    )
    attended_low = attended.reshape(2 * SEG, HQ).astype(jnp.bfloat16)
    branch_attn = jnp.dot(attended_low, full_merge, preferred_element_type=jnp.float32)
    hidden = rows_in + rmsnorm(branch_attn, gain_second)
    normed_mid = rmsnorm(hidden, gain_third).astype(jnp.bfloat16)
    gate_up = jnp.dot(normed_mid, full_expand, preferred_element_type=jnp.float32)
    activated = gated_gelu(gate_up).astype(jnp.bfloat16)
    branch_ff = jnp.dot(activated, full_reduce, preferred_element_type=jnp.float32)
    result = hidden + rmsnorm(branch_ff, gain_fourth)
    block_output = result.astype(jnp.bfloat16).reshape(1, 2, SEG, D)
    upstream = cotangent[0].reshape(2 * SEG, D).astype(jnp.float32)
    _, outer_back = jax.vjp(rmsnorm, branch_ff, gain_fourth)
    branch_grad, grad_fourth = outer_back(upstream)
    branch_low = branch_grad.astype(jnp.bfloat16)
    grad_reduce = contract_rows(activated, branch_low)
    active_grad = contract_cols(branch_low, full_reduce)
    _, gelu_back = jax.vjp(gated_gelu, gate_up)
    (expand_grad,) = gelu_back(active_grad)
    expand_low = expand_grad.astype(jnp.bfloat16)
    grad_expand = contract_rows(normed_mid, expand_low)
    middle_grad = contract_cols(expand_low, full_expand)
    _, third_back = jax.vjp(rmsnorm, hidden, gain_third)
    hidden_part, grad_third = third_back(middle_grad)
    hidden_grad = upstream + hidden_part
    _, second_back = jax.vjp(rmsnorm, branch_attn, gain_second)
    attn_grad, grad_second = second_back(hidden_grad)
    attn_low = attn_grad.astype(jnp.bfloat16)
    grad_merge = contract_rows(attended_low, attn_low)
    context_reduced = (
        contract_cols(attn_low, full_merge).astype(jnp.bfloat16).reshape(2, SEG, NH, HD)
    )
    attention_probabilities = jnp.exp(score_block() - log_total)
    probability_recomputed = attention_probabilities.astype(jnp.bfloat16)
    value_grad = jnp.einsum(
        "jsze,jzsf->jef",
        probability_recomputed,
        context_reduced,
        preferred_element_type=jnp.float32,
    )
    chance_grad = jnp.einsum(
        "itge,iue->igtu", context_reduced, value_reduced, preferred_element_type=jnp.float32
    )
    inner_sum = jnp.sum(attention_probabilities * chance_grad, axis=-1, keepdims=True)
    score_reduced = (attention_probabilities * (chance_grad - inner_sum)).astype(jnp.bfloat16)
    query_grad = jnp.einsum(
        "ayco,aox->acyx", score_reduced, key_reduced, preferred_element_type=jnp.float32
    )
    key_grad = jnp.einsum(
        "jsze,jzsf->jef", score_reduced, query_reduced, preferred_element_type=jnp.float32
    )
    pair_grad = jnp.concatenate([key_grad, value_grad], axis=-1)
    spread = jnp.zeros((WINDOW + prompt_size, 2 * HD), jnp.float32)
    spread = lax.dynamic_update_slice_in_dim(spread, pair_grad[0], block_index * SEG, 0)
    spread = jnp.concatenate(
        [spread[:prompt_size], spread[prompt_size:] + pair_grad[1, :WINDOW]], axis=0
    )
    owned_pairs = lax.psum_scatter(
        spread[WINDOW:].astype(jnp.bfloat16), "blk", scatter_dimension=0, tiled=True
    ).astype(jnp.float32)
    pair_rows = jnp.concatenate([owned_pairs, pair_grad[1, WINDOW:]], axis=0)

    def head_section(mixed_rows, query_gain, key_gain):
        return prepare_heads(mixed_rows, query_gain, key_gain, cosine, sine_part)

    _, heads_back = jax.vjp(head_section, projected, gain_query, gain_key)
    mixed_grad, grad_query, grad_key = heads_back(
        (query_grad.reshape(2 * SEG, NH, HD), pair_rows[:, :HD], pair_rows[:, HD:])
    )
    mixed_low = mixed_grad.astype(jnp.bfloat16)
    grad_attend = contract_rows(normed_low, mixed_low)
    normed_grad = contract_cols(mixed_low, full_attend)
    _, first_back = jax.vjp(rmsnorm, rows_in, gain_first)
    input_part, grad_first = first_back(normed_grad)
    input_grad = (hidden_grad + input_part).reshape(1, 2, SEG, D)
    gain_grads = jnp.concatenate(
        [grad_first, grad_second, grad_third, grad_fourth, grad_query, grad_key]
    )
    owned_attend, owned_merge, owned_expand, owned_reduce, owned_gains = (
        lax.psum_scatter(
            grad_attend.astype(jnp.bfloat16), "blk", scatter_dimension=0, tiled=True
        ).astype(jnp.float32),
        lax.psum_scatter(
            grad_merge.astype(jnp.bfloat16), "blk", scatter_dimension=0, tiled=True
        ).astype(jnp.float32),
        lax.psum_scatter(
            grad_expand.astype(jnp.bfloat16), "blk", scatter_dimension=0, tiled=True
        ).astype(jnp.float32),
        lax.psum_scatter(
            grad_reduce.astype(jnp.bfloat16), "blk", scatter_dimension=0, tiled=True
        ).astype(jnp.float32),
        lax.psum_scatter(
            gain_grads.astype(jnp.bfloat16), "blk", scatter_dimension=0, tiled=True
        ).astype(jnp.float32),
    )
    owned_all = (owned_attend, owned_merge, owned_expand, owned_reduce)
    buffers = (error_attend, error_merge, error_expand, error_reduce)
    factors = (start_attend, start_merge, start_expand, start_reduce)
    combined = [owned + ERROR_KEEP * buffer[0] for owned, buffer in zip(owned_all, buffers)]
    lefts = [
        jnp.dot(matrix, factor[0], precision=lax.Precision.HIGHEST)
        for matrix, factor in zip(combined, factors)
    ]
    left_sums = lax.psum((lefts[0], lefts[1], lefts[2], lefts[3], owned_gains), "grp")
    basis_set = [orthonormal(left_sums[member]) for member in range(4)]
    rights = [
        lax.dot_general(matrix, basis, (((0,), (0,)), ((), ())), precision=lax.Precision.HIGHEST)
        for matrix, basis in zip(combined, basis_set)
    ]
    right_sums = (
        lax.psum(rights[0].astype(jnp.bfloat16), "grp").astype(jnp.float32),
        lax.psum(rights[1].astype(jnp.bfloat16), "grp").astype(jnp.float32),
        lax.psum(rights[2].astype(jnp.bfloat16), "grp").astype(jnp.float32),
        lax.psum(rights[3].astype(jnp.bfloat16), "grp").astype(jnp.float32),
    )
    residues = [
        matrix - jnp.dot(basis, partial_right.T, precision=lax.Precision.HIGHEST)
        for matrix, basis, partial_right in zip(combined, basis_set, rights)
    ]
    directions = [
        jnp.dot(basis, summed.T, precision=lax.Precision.HIGHEST) / groups
        for basis, summed in zip(basis_set, right_sums)
    ]
    directions.append(left_sums[4] / groups)
    moments = (moment_attend, moment_merge, moment_expand, moment_reduce, moment_gains)
    masters = (master_attend, master_merge, master_expand, master_reduce, master_gains)
    velocities = [
        MOMENTUM * moment + (1.0 - MOMENTUM) * direction
        for moment, direction in zip(moments, directions)
    ]
    updated = [master - STEP_RATE * velocity for master, velocity in zip(masters, velocities)]
    return (
        block_output,
        input_grad,
        owned_attend[None],
        owned_merge[None],
        owned_expand[None],
        owned_reduce[None],
        owned_gains[None],
        basis_set[0],
        basis_set[1],
        basis_set[2],
        basis_set[3],
        right_sums[0][None],
        right_sums[1][None],
        right_sums[2][None],
        right_sums[3][None],
        residues[0][None],
        residues[1][None],
        residues[2][None],
        residues[3][None],
        velocities[0],
        velocities[1],
        velocities[2],
        velocities[3],
        velocities[4],
        updated[0],
        updated[1],
        updated[2],
        updated[3],
        updated[4],
        updated[0].astype(jnp.bfloat16),
        updated[1].astype(jnp.bfloat16),
        updated[2].astype(jnp.bfloat16),
        updated[3].astype(jnp.bfloat16),
        updated[4].astype(jnp.bfloat16),
    )


def solution(mesh):
    in_specs = (
        P("grp", None, "blk", None),
        P("grp", None, "blk", None),
        P("blk", None),
        P("blk", None),
        P("blk", None),
        P("blk", None),
        P("blk"),
        P("blk", None),
        P("blk", None),
        P("blk", None),
        P("blk", None),
        P("blk"),
        P("grp", "blk", None),
        P("grp", "blk", None),
        P("grp", "blk", None),
        P("grp", "blk", None),
        P("blk", None, None),
        P("blk", None, None),
        P("blk", None, None),
        P("blk", None, None),
    )
    out_specs = (
        P("grp", None, "blk", None),
        P("grp", None, "blk", None),
        P("grp", "blk", None),
        P("grp", "blk", None),
        P("grp", "blk", None),
        P("grp", "blk", None),
        P("grp", "blk"),
        P("blk", None),
        P("blk", None),
        P("blk", None),
        P("blk", None),
        P("blk", None, None),
        P("blk", None, None),
        P("blk", None, None),
        P("blk", None, None),
        P("grp", "blk", None),
        P("grp", "blk", None),
        P("grp", "blk", None),
        P("grp", "blk", None),
        P("blk", None),
        P("blk", None),
        P("blk", None),
        P("blk", None),
        P("blk"),
        P("blk", None),
        P("blk", None),
        P("blk", None),
        P("blk", None),
        P("blk"),
        P("blk", None),
        P("blk", None),
        P("blk", None),
        P("blk", None),
        P("blk"),
    )
    return jax.shard_map(
        on_device, mesh=mesh, in_specs=in_specs, out_specs=out_specs, check_vma=False
    )
```

profile of v0, /device:TPU:0, one launch (start us, length us, event | category | flops | bytes accessed | tf_op | source)
XLA Modules:
  0.0 946.2 jit_solution(14591315327089073494)
XLA Ops:
  10.2 14.9 %all-gather = bf16[4,1,768]{2,1,0:T(2,128)(2,1)S(1)} all-gather(bf16[1,1,768]{2,1,0:T(2,128)(2,1)S(1)} %reshape.422), channel_id=1, replica_groups=mesh['grp'=8,'blk'=4] {'blk'}, dimensions={0}, use_global_device_ids=true | all-gather | bytes 7680 | tf_op jit(solution)/shard_map/all_gather | solution.py:112
  27.0 29.5 %all-gather.7.cloned.1.call-done = bf16[640,1536]{1,0:T(8,128)(2,1)} async-done(((bf16[160,1536]{1,0:T(8,128)(2,1)}), bf16[640,1536]{1,0:T(8,128)(2,1)}) %all-gather.7.cloned.1.call-update) | async-done | bytes 1966096 | tf_op jit(solution)/shard_map/all_gather | solution.py:108
  83.9 6.4 all-gather.9.cloned.1.call-done
  98.5 25.9 %all-gather.11.cloned.1.call-done = bf16[1024,640]{1,0:T(8,128)(2,1)} async-done(((bf16[256,640]{1,0:T(8,128)(2,1)}), bf16[1024,640]{1,0:T(8,128)(2,1)}) %all-gather.11.cloned.1.call-update) | async-done | bytes 1310736 | tf_op jit(solution)/shard_map/all_gather | solution.py:109
  127.8 95.7 %all-gather.13.cloned.1.call-done = bf16[640,4096]{1,0:T(8,128)(2,1)} async-done(((bf16[160,4096]{1,0:T(8,128)(2,1)}), bf16[640,4096]{1,0:T(8,128)(2,1)}) %all-gather.13.cloned.1.call-update) | async-done | bytes 5242896 | tf_op jit(solution)/shard_map/all_gather | solution.py:110
  235.0 43.6 %all-gather.15.cloned.1.call-done = bf16[2048,640]{1,0:T(8,128)(2,1)} async-done(((bf16[512,640]{1,0:T(8,128)(2,1)}), bf16[2048,640]{1,0:T(8,128)(2,1)}) %all-gather.15.cloned.1.call-update) | async-done | bytes 2621456 | tf_op jit(solution)/shard_map/all_gather | solution.py:111
  334.8 10.6 %reduce-scatter.6.cloned.1.call-done = bf16[256,512]{1,0:T(8,128)(2,1)} async-done(((bf16[1024,512]{1,0:T(8,128)(2,1)}), bf16[256,512]{1,0:T(8,128)(2,1)}) %reduce-scatter.6.cloned.1.call-update) | async-done | bytes 262160 | tf_op jit(solution)/shard_map/reduce_scatter | solution.py:221
  363.3 8.8 convolution_convert_fusion
  380.2 9.7 %all-reduce.10 = bf16[3072]{0:T(1024)(128)(2,1)S(1)} all-reduce(bf16[3072]{0:T(1024)(128)(2,1)S(1)} %dynamic-update-slice.5), channel_id=7, replica_groups=mesh['grp'=8,'blk'=4] {'blk'}, use_global_device_ids=true, to_apply=%region_26.27.clone | all-reduce | flops 3072 | bytes 12288
  396.9 35.1 %reduce-scatter.14.cloned.1.call-done = bf16[512,640]{1,0:T(8,128)(2,1)} async-done(((bf16[2048,640]{1,0:T(8,128)(2,1)}), bf16[512,640]{1,0:T(8,128)(2,1)}) %reduce-scatter.14.cloned.1.call-update) | async-done | bytes 655376 | tf_op jit(solution)/shard_map/reduce_scatter | solution.py:252
  437.1 39.0 %reduce-scatter.8.cloned.1.call-done = bf16[160,1536]{1,0:T(8,128)(2,1)} async-done(((bf16[640,1536]{1,0:T(8,128)(2,1)}), bf16[160,1536]{1,0:T(8,128)(2,1)}) %reduce-scatter.8.cloned.1.call-update) | async-done | bytes 491536 | tf_op jit(solution)/shard_map/reduce_scatter | solution.py:243
  480.5 90.7 %reduce-scatter.12.cloned.1.call-done = bf16[160,4096]{1,0:T(8,128)(2,1)} async-done(((bf16[640,4096]{1,0:T(8,128)(2,1)}), bf16[160,4096]{1,0:T(8,128)(2,1)}) %reduce-scatter.12.cloned.1.call-update) | async-done | bytes 1310736 | tf_op jit(solution)/shard_map/reduce_scatter | solution.py:249
  574.7 25.0 %all-reduce.11 = (f32[160,8]{0,1:T(8,128)S(1)}, f32[256,8]{0,1:T(8,128)S(1)}, f32[160,8]{0,1:T(8,128)S(1)}, f32[512,8]{0,1:T(8,128)S(1)}, f32[768]{0:T(1024)}) all-reduce(f32[160,8]{0,1:T(8,128)S(1)} %fusion.88, f32[256,8]{0,1:T(8,128)S(1)} %fusion.92, f32[160,8]{0,1:T(8,128)S(1)} %fusion.66, ...), channel_id=1, replica_groups=mesh['grp'=8,'blk'=4] {'grp'}, use_global_device_ids=true, to_apply=%region_27.28 | all-reduce | flops 9472 | bytes 75776 | tf_op jit(solution)/shard_map/psum | solution.py:267
  613.2 6.4 multiply_reduce_fusion.125
  642.2 18.1 %subtract_multiply_fusion.21 = (f32[160,1]{0,1:T(1,128)S(1)}, f32[160,1]{0,1:T(1,128)S(1)}, f32[160,1]{0,1:T(1,128)S(1)}, f32[160,1]{0,1:T(1,128)S(1)}, f32[160,...) fusion(f32[160,1]{0,1:T(1,128)S(1)} %get-tuple-element.344, f32[]{:T(128)S(6)} %rsqrt.180, ...), kind=kLoop, calls=%fused_computation.453 | loop fusion | flops 10080 | bytes 9740 | tf_op jit(solution)/shard_map/mul | solution.py:65
  673.9 6.4 multiply_reduce_fusion.89
  702.9 18.1 %subtract_multiply_fusion.14 = (f32[256,1]{0,1:T(1,128)S(1)}, f32[256,1]{0,1:T(1,128)S(1)}, f32[256,1]{0,1:T(1,128)S(1)}, f32[256,1]{0,1:T(1,128)S(1)}, f32[256,...) fusion(f32[256,1]{0,1:T(1,128)S(1)} %get-tuple-element.336, f32[]{:T(128)S(6)} %rsqrt.188, ...), kind=kLoop, calls=%fused_computation.383 | loop fusion | flops 16128 | bytes 15500 | tf_op jit(solution)/shard_map/mul | solution.py:65
  734.5 6.4 multiply_reduce_fusion.53
  763.4 18.5 %subtract_multiply_fusion.7 = (f32[160,1]{0,1:T(1,128)}, f32[160,1]{0,1:T(1,128)}, f32[160,1]{0,1:T(1,128)}, f32[160,1]{0,1:T(1,128)}, f32[160,1]{0,1:T(1,128)}, /*index=5*/f32[160,1]{0,1:T(1,128)}, f32[160,1]{0,1:T(1,128)}) fusion(f32[160,1]{0,1:T(1,128)S(1)} %get-tuple-element.328, f32[]{:T(128)S(6)} %rsqrt.196, f32[]{:T(128)} %get-tuple-element.208, ...), kind=kLoop, calls=%fused_computation.313 | loop fusion | flops 10080 | bytes 9740 | tf_op jit(solution)/shard_map/mul | solution.py:65
  795.4 6.4 multiply_reduce_fusion.17
  825.5 18.0 %subtract_multiply_fusion = (f32[512,1]{0,1:T(1,128)S(1)}, f32[512,1]{0,1:T(1,128)S(1)}, f32[512,1]{0,1:T(1,128)S(1)}, f32[512,1]{0,1:T(1,128)S(1)}, f32[512,1]{...) fusion(f32[512,1]{0,1:T(1,128)S(1)} %get-tuple-element.314, f32[]{:T(128)S(6)} %rsqrt.204, ...), kind=kLoop, calls=%fused_computation.222 | loop fusion | flops 32256 | bytes 30860 | tf_op jit(solution)/shard_map/mul | solution.py:65
  850.3 23.6 %all-reduce.12 = (bf16[1536,8]{0,1:T(8,128)(2,1)S(1)}, bf16[640,8]{0,1:T(8,128)(2,1)S(1)}, bf16[640,8]{0,1:T(8,128)(2,1)}) all-reduce(bf16[1536,8]{0,1:T(8,128)(2,1)S(1)} %get-tuple-element.361, bf16[640,8]{0,1:T(8,128)(2,1)S(1)} %get-tuple-element.363, ...), channel_id=1, replica_groups=mesh['grp'=8,'blk'=4] {'grp'}, use_global_device_ids=true, to_apply=%region_175.176 | all-reduce | flops 22528 | bytes 90112 | tf_op jit(solution)/shard_map/psum | solution.py:274
  902.0 29.5 %all-reduce.15.cloned.1.call-done = bf16[4096,8]{0,1:T(8,128)(2,1)} async-done(((bf16[4096,8]{0,1:T(8,128)(2,1)}), bf16[4096,8]{0,1:T(8,128)(2,1)}) %all-reduce.15.cloned.1.call-update) | async-done | bytes 65552 | tf_op jit(solution)/shard_map/psum | solution.py:276
  933.1 6.3 fusion.127
  (479 shorter events, 314.8 us)
Async XLA Ops:
  7.2 564.0 %copy-start = (f32[1,4096,8]{1,2,0:T(8,128)S(1)}, f32[1,4096,8]{1,2,0:T(8,128)}, u32[]{:S(2)}) copy-start(f32[1,4096,8]{1,2,0:T(8,128)} %param.38) | copy-start | bytes 393220
  7.2 49.2 %all-gather.7.cloned.1.call-start = ((), (), s32[]{:S(2)}) async-start(), calls=%async_computation.5 | async-start | bytes 2457600 | tf_op jit(solution)/shard_map/all_gather | solution.py:108
  9.4 80.9 %all-gather.9.cloned.1.call-start = ((), (), s32[]{:S(2)}) async-start(), calls=%async_computation.6 | async-start | bytes 1310720 | tf_op jit(solution)/shard_map/all_gather | solution.py:133
  26.0 34.4 %copy-start.88 = (f32[256]{0:T(256)}, f32[256]{0:T(256)S(1)}, u32[]{:S(2)}) copy-start(f32[256]{0:T(256)S(1)} %get-tuple-element.325) | copy-start | bytes 3076
  26.6 100.8 %copy-start.77 = (f32[640]{0:T(1024)}, f32[640]{0:T(1024)S(1)}, u32[]{:S(2)}) copy-start(f32[640]{0:T(1024)S(1)} %get-tuple-element.323) | copy-start | bytes 7684
  26.7 33.6 %copy-start.42 = (f32[512,128]{1,0:T(8,128)}, f32[512,128]{1,0:T(8,128)S(1)}, u32[]{:S(2)}) copy-start(f32[512,128]{1,0:T(8,128)S(1)} %broadcast_multiply_fusion.1) | copy-start | bytes 786436
  27.0 32.4 %copy-start.55 = (bf16[512,640]{1,0:T(8,128)(2,1)}, bf16[512,640]{1,0:T(8,128)(2,1)S(1)}, u32[]{:S(2)}) copy-start(bf16[512,640]{1,0:T(8,128)(2,1)S(1)} %fusion.45) | copy-start | bytes 1966084
  63.3 61.0 %all-gather.11.cloned.1.call-start = ((), (), s32[]{:S(2)}) async-start(), calls=%async_computation.7 | async-start | bytes 1638400 | tf_op jit(solution)/shard_map/all_gather | solution.py:109
  65.3 158.3 %all-gather.13.cloned.1.call-start = ((), (), s32[]{:S(2)}) async-start(), calls=%async_computation.8 | async-start | bytes 6553600 | tf_op jit(solution)/shard_map/all_gather | solution.py:110
  66.6 212.1 %all-gather.15.cloned.1.call-start = ((), (), s32[]{:S(2)}) async-start(), calls=%async_computation.9 | async-start | bytes 3276800 | tf_op jit(solution)/shard_map/all_gather | solution.py:111
  68.8 276.7 %reduce-scatter.6.cloned.1.call-start = ((), (), s32[]{:S(2)}) async-start(), calls=%async_computation.10 | async-start | bytes 1310720 | tf_op jit(solution)/shard_map/reduce_scatter | solution.py:221
  235.0 48.0 %copy-start.34 = (bf16[1,2,256,640]{3,2,1,0:T(8,128)(2,1)S(1)}, bf16[1,2,256,640]{3,2,1,0:T(8,128)(2,1)}, u32[]{:S(2)}) copy-start(bf16[1,2,256,640]{3,2,1,0:T(8,128)(2,1)} %param.21) | copy-start | bytes 1966084
  235.0 48.0 %copy-start.87 = (f32[640]{0:T(1024)S(1)}, f32[640]{0:T(1024)}, u32[]{:S(2)}) copy-start(f32[640]{0:T(1024)} %get-tuple-element.321) | copy-start | bytes 7684
  319.2 74.2 %reduce-scatter.10.cloned.1.call-start = ((), (), s32[]{:S(2)}) async-start(), calls=%async_computation.12 | async-start | bytes 1638400 | tf_op jit(solution)/shard_map/reduce_scatter | solution.py:246
  322.9 109.1 %reduce-scatter.14.cloned.1.call-start = ((), (), s32[]{:S(2)}) async-start(), calls=%async_computation.14 | async-start | bytes 3276800 | tf_op jit(solution)/shard_map/reduce_scatter | solution.py:252
  327.5 148.7 %reduce-scatter.8.cloned.1.call-start = ((), (), s32[]{:S(2)}) async-start(), calls=%async_computation.11 | async-start | bytes 2457600 | tf_op jit(solution)/shard_map/reduce_scatter | solution.py:243
  363.2 208.0 %reduce-scatter.12.cloned.1.call-start = ((), (), s32[]{:S(2)}) async-start(), calls=%async_computation.13 | async-start | bytes 6553600 | tf_op jit(solution)/shard_map/reduce_scatter | solution.py:249
  372.2 559.3 %all-reduce.15.cloned.1.call-start = ((), (), s32[]{:S(2)}) async-start(), calls=%async_computation.15 | async-start | bytes 131072 | tf_op jit(solution)/shard_map/psum | solution.py:276
  393.4 40.9 %copy-start.92 = (f32[1,640,8]{1,2,0:T(8,128)S(1)}, f32[1,640,8]{1,2,0:T(8,128)}, u32[]{:S(2)}) copy-start(f32[1,640,8]{1,2,0:T(8,128)} %param.39) | copy-start | bytes 61444
  396.9 79.2 %copy-start.81 = (f32[1,1536,8]{1,2,0:T(8,128)S(1)}, f32[1,1536,8]{1,2,0:T(8,128)}, u32[]{:S(2)}) copy-start(f32[1,1536,8]{1,2,0:T(8,128)} %param.36) | copy-start | bytes 147460
  434.3 136.9 %copy-start.6 = (f32[1,160,4096]{2,1,0:T(8,128)S(1)}, f32[1,160,4096]{2,1,0:T(8,128)}, u32[]{:S(2)}) copy-start(f32[1,160,4096]{2,1,0:T(8,128)} %param.34) | copy-start | bytes 7864324
  843.6 54.4 %copy-start.62 = (f32[512,8]{0,1:T(8,128)}, f32[512,8]{0,1:T(8,128)S(1)}, u32[]{:S(2)}) copy-start(f32[512,8]{0,1:T(8,128)S(1)} %stack.26) | copy-start | bytes 49156
  898.0 35.0 %copy-start.21 = (f32[160,4096]{1,0:T(8,128)S(1)}, f32[160,4096]{1,0:T(8,128)}, u32[]{:S(2)}) copy-start(f32[160,4096]{1,0:T(8,128)} %param.24) | copy-start | bytes 7864324
  898.0 35.0 %copy-start.69 = (f32[160,8]{0,1:T(8,128)S(1)}, f32[160,8]{0,1:T(8,128)}, u32[]{:S(2)}) copy-start(f32[160,8]{0,1:T(8,128)} %stack.25) | copy-start | bytes 15364
  (113 other events, 729.4 us)
Sparse Core Ops, SparseCore 0:
  10.2 46.2 all-gather.6
  63.5 26.7 all-gather.8
  92.4 31.8 all-gather.10
  126.4 97.1 all-gather.12
  225.5 53.0 all-gather.14
  319.4 26.0 reduce-scatter.5
  348.3 29.8 reduce-scatter.9
  381.1 50.8 reduce-scatter.13
  434.9 41.1 reduce-scatter.7
  478.3 92.8 reduce-scatter.11
  879.6 51.8 all-reduce.14
where the time goes:
time: 953 us; the launch traced here: 946 us
  waiting for transfers between devices  406 us (43%)
  other arithmetic  282 us (30%)
  matrix products  110 us (12%)
  blocking collectives  73.2 us (8%)
  between operations  38.5 us (4%)
  local copies, waits for them, and re-layouts  35.1 us (4%)
    reduce_sum x40, other arithmetic, orthonormal(): vector = vector - jnp.sum(basis * vector) * basis  118 us
    all_gather x1, waiting for transfers between devices, on_device(): lax.all_gather(master_expand.astype(jnp.bfloat16), 'blk', axis=0, tiled=T...  95.7 us
    reduce_scatter x1, waiting for transfers between devices, on_device(): lax.psum_scatter(grad_expand.astype(jnp.bfloat16), 'blk', scatter_dimensi...  90.7 us
    mul x4, other arithmetic, orthonormal(): columns.append(vector * lax.rsqrt(jnp.sum(vector * vector) + NORM_EPS))  72.7 us
    all_gather x1, waiting for transfers between devices, on_device(): lax.all_gather(master_reduce.astype(jnp.bfloat16), 'blk', axis=0, tiled=T...  43.6 us
    reduce_scatter x1, waiting for transfers between devices, on_device(): lax.psum_scatter(grad_attend.astype(jnp.bfloat16), 'blk', scatter_dimensi...  39 us
    reduce_scatter x1, waiting for transfers between devices, on_device(): lax.psum_scatter(grad_reduce.astype(jnp.bfloat16), 'blk', scatter_dimensi...  35.1 us
    reduce_sum x20, other arithmetic, orthonormal(): columns.append(vector * lax.rsqrt(jnp.sum(vector * vector) + NORM_EPS))  30.8 us
  transfers between devices with their start and end apart: 11, of which 10 were waited for; matrix products, arithmetic and copies ran while one was open for 12% of the time, Pallas kernels for 0%

commit v1 on v0

--- a/solution.py
+++ b/solution.py
@@ -1,3 +1,4 @@
+import functools
 import jax
 import jax.numpy as jnp
 from jax import lax
@@ -16,6 +17,14 @@
 MOMENTUM = 0.9
 STEP_RATE = 0.02
 NEG_FILL = -1e30
+
+
+def convert_keys_on(local, peer_axis):
+    fresh = lax.all_gather(local, peer_axis)
+    return jnp.sum(fresh, axis=0)
+
+
+state_sheet = functools.partial(convert_keys_on, peer_axis="grp")
 
 
 def rmsnorm(values, gain_row):
@@ -273,7 +282,7 @@
     right_sums = (
         lax.psum(rights[0].astype(jnp.bfloat16), "grp").astype(jnp.float32),
         lax.psum(rights[1].astype(jnp.bfloat16), "grp").astype(jnp.float32),
-        lax.psum(rights[2].astype(jnp.bfloat16), "grp").astype(jnp.float32),
+        state_sheet(rights[2].astype(jnp.bfloat16)).astype(jnp.float32),
         lax.psum(rights[3].astype(jnp.bfloat16), "grp").astype(jnp.float32),
     )
     residues = [

time: 953 us -> 935 us (0.981)
  waiting for transfers between devices: 406 us -> 377 us
  blocking collectives: 73.2 us -> 83.7 us
    psum x1 -> x0, waiting for transfers between devices: 29.5 us -> none  [on_device(): lax.psum(rights[2].astype(jnp.bfloat16), 'grp').astype(jnp.float32)]
    all_gather x0 -> x1, blocking collectives: none -> 9.91 us  [convert_keys_on(): fresh = lax.all_gather(local, peer_axis)]
    unnamed x261 -> x243, local copies, waits for them, and re-layouts: 20 us -> 19.9 us
  transfers between devices with their start and end apart: 11 -> 10, of which waited for: 10 -> 9; matrix products, arithmetic and copies ran while one was open for 12% -> 10% of each run, Pallas kernels for 0% -> 0%
where the time goes in v1:
time: 935 us; the launch traced here: 927 us
  waiting for transfers between devices  377 us (40%)
  other arithmetic  283 us (30%)
  matrix products  108 us (12%)
  blocking collectives  83.7 us (9%)
  between operations  38.7 us (4%)
  local copies, waits for them, and re-layouts  36.6 us (4%)
    reduce_sum x40, other arithmetic, orthonormal(): vector = vector - jnp.sum(basis * vector) * basis  118 us
    all_gather x1, waiting for transfers between devices, on_device(): lax.all_gather(master_expand.astype(jnp.bfloat16), 'blk', axis=0, tiled=T...  95.7 us
    reduce_scatter x1, waiting for transfers between devices, on_device(): lax.psum_scatter(grad_expand.astype(jnp.bfloat16), 'blk', scatter_dimensi...  90.7 us
    mul x4, other arithmetic, orthonormal(): columns.append(vector * lax.rsqrt(jnp.sum(vector * vector) + NORM_EPS))  73.3 us
    all_gather x1, waiting for transfers between devices, on_device(): lax.all_gather(master_reduce.astype(jnp.bfloat16), 'blk', axis=0, tiled=T...  43.6 us
    reduce_scatter x1, waiting for transfers between devices, on_device(): lax.psum_scatter(grad_attend.astype(jnp.bfloat16), 'blk', scatter_dimensi...  39 us
    reduce_scatter x1, waiting for transfers between devices, on_device(): lax.psum_scatter(grad_reduce.astype(jnp.bfloat16), 'blk', scatter_dimensi...  35.1 us
    reduce_sum x20, other arithmetic, orthonormal(): columns.append(vector * lax.rsqrt(jnp.sum(vector * vector) + NORM_EPS))  30.7 us
  transfers between devices with their start and end apart: 10, of which 9 were waited for; matrix products, arithmetic and copies ran while one was open for 10% of the time, Pallas kernels for 0%

profile of v1, /device:TPU:0, one launch (start us, length us, event | category | flops | bytes accessed | tf_op | source)
XLA Modules:
  0.0 927.2 jit_solution(7239983367907526645)
XLA Ops:
  10.2 14.9 %all-gather.1 = bf16[4,1,768]{2,1,0:T(2,128)(2,1)S(1)} all-gather(bf16[1,1,768]{2,1,0:T(2,128)(2,1)S(1)} %reshape.432), channel_id=1, replica_groups=mesh['grp'=8,'blk'=4] {'blk'}, dimensions={0}, use_global_device_ids=true | all-gather | bytes 7680 | tf_op jit(solution)/shard_map/all_gather | solution.py:121
  27.0 29.5 %all-gather.8.cloned.1.call-done = bf16[640,1536]{1,0:T(8,128)(2,1)} async-done(((bf16[160,1536]{1,0:T(8,128)(2,1)}), bf16[640,1536]{1,0:T(8,128)(2,1)}) %all-gather.8.cloned.1.call-update) | async-done | bytes 1966096 | tf_op jit(solution)/shard_map/all_gather | solution.py:117
  83.9 6.4 all-gather.10.cloned.1.call-done
  98.5 25.9 %all-gather.12.cloned.1.call-done = bf16[1024,640]{1,0:T(8,128)(2,1)} async-done(((bf16[256,640]{1,0:T(8,128)(2,1)}), bf16[1024,640]{1,0:T(8,128)(2,1)}) %all-gather.12.cloned.1.call-update) | async-done | bytes 1310736 | tf_op jit(solution)/shard_map/all_gather | solution.py:118
  127.8 95.7 %all-gather.14.cloned.1.call-done = bf16[640,4096]{1,0:T(8,128)(2,1)} async-done(((bf16[160,4096]{1,0:T(8,128)(2,1)}), bf16[640,4096]{1,0:T(8,128)(2,1)}) %all-gather.14.cloned.1.call-update) | async-done | bytes 5242896 | tf_op jit(solution)/shard_map/all_gather | solution.py:119
  223.5 5.5 fusion.123
  235.0 43.6 %all-gather.16.cloned.1.call-done = bf16[2048,640]{1,0:T(8,128)(2,1)} async-done(((bf16[512,640]{1,0:T(8,128)(2,1)}), bf16[2048,640]{1,0:T(8,128)(2,1)}) %all-gather.16.cloned.1.call-update) | async-done | bytes 2621456 | tf_op jit(solution)/shard_map/all_gather | solution.py:120
  334.8 10.6 %reduce-scatter.6.cloned.1.call-done = bf16[256,512]{1,0:T(8,128)(2,1)} async-done(((bf16[1024,512]{1,0:T(8,128)(2,1)}), bf16[256,512]{1,0:T(8,128)(2,1)}) %reduce-scatter.6.cloned.1.call-update) | async-done | bytes 262160 | tf_op jit(solution)/shard_map/reduce_scatter | solution.py:230
  363.3 8.8 convolution_convert_fusion
  380.2 9.7 %all-reduce.10 = bf16[3072]{0:T(1024)(128)(2,1)S(1)} all-reduce(bf16[3072]{0:T(1024)(128)(2,1)S(1)} %dynamic-update-slice.5), channel_id=8, replica_groups=mesh['grp'=8,'blk'=4] {'blk'}, use_global_device_ids=true, to_apply=%region_26.27.clone | all-reduce | flops 3072 | bytes 12288
  396.9 35.1 %reduce-scatter.14.cloned.1.call-done = bf16[512,640]{1,0:T(8,128)(2,1)} async-done(((bf16[2048,640]{1,0:T(8,128)(2,1)}), bf16[512,640]{1,0:T(8,128)(2,1)}) %reduce-scatter.14.cloned.1.call-update) | async-done | bytes 655376 | tf_op jit(solution)/shard_map/reduce_scatter | solution.py:261
  437.1 39.0 %reduce-scatter.8.cloned.1.call-done = bf16[160,1536]{1,0:T(8,128)(2,1)} async-done(((bf16[640,1536]{1,0:T(8,128)(2,1)}), bf16[160,1536]{1,0:T(8,128)(2,1)}) %reduce-scatter.8.cloned.1.call-update) | async-done | bytes 491536 | tf_op jit(solution)/shard_map/reduce_scatter | solution.py:252
  480.5 90.7 %reduce-scatter.12.cloned.1.call-done = bf16[160,4096]{1,0:T(8,128)(2,1)} async-done(((bf16[640,4096]{1,0:T(8,128)(2,1)}), bf16[160,4096]{1,0:T(8,128)(2,1)}) %reduce-scatter.12.cloned.1.call-update) | async-done | bytes 1310736 | tf_op jit(solution)/shard_map/reduce_scatter | solution.py:258
  574.7 25.0 %all-reduce.11 = (f32[160,8]{0,1:T(8,128)S(1)}, f32[256,8]{0,1:T(8,128)S(1)}, f32[160,8]{0,1:T(8,128)S(1)}, f32[512,8]{0,1:T(8,128)S(1)}, f32[768]{0:T(1024)}) all-reduce(f32[160,8]{0,1:T(8,128)S(1)} %fusion.88, f32[256,8]{0,1:T(8,128)S(1)} %fusion.92, f32[160,8]{0,1:T(8,128)S(1)} %fusion.66, ...), channel_id=1, replica_groups=mesh['grp'=8,'blk'=4] {'grp'}, use_global_device_ids=true, to_apply=%region_27.28 | all-reduce | flops 9472 | bytes 75776 | tf_op jit(solution)/shard_map/psum | solution.py:276
  613.2 6.4 multiply_reduce_fusion.125
  642.2 18.1 %subtract_multiply_fusion.21 = (f32[160,1]{0,1:T(1,128)S(1)}, f32[160,1]{0,1:T(1,128)S(1)}, f32[160,1]{0,1:T(1,128)S(1)}, f32[160,1]{0,1:T(1,128)S(1)}, f32[160,...) fusion(f32[160,1]{0,1:T(1,128)S(1)} %get-tuple-element.344, f32[]{:T(128)S(6)} %rsqrt.180, ...), kind=kLoop, calls=%fused_computation.453 | loop fusion | flops 10080 | bytes 9740 | tf_op jit(solution)/shard_map/mul | solution.py:74
  673.9 6.4 multiply_reduce_fusion.89
  702.8 18.6 %subtract_multiply_fusion.14 = (f32[256,1]{0,1:T(1,128)S(1)}, f32[256,1]{0,1:T(1,128)S(1)}, f32[256,1]{0,1:T(1,128)S(1)}, f32[256,1]{0,1:T(1,128)S(1)}, f32[256,...) fusion(f32[256,1]{0,1:T(1,128)S(1)} %get-tuple-element.336, f32[]{:T(128)S(6)} %rsqrt.188, ...), kind=kLoop, calls=%fused_computation.383 | loop fusion | flops 16128 | bytes 15500 | tf_op jit(solution)/shard_map/mul | solution.py:74
  734.9 6.4 multiply_reduce_fusion.53
  763.8 18.5 %subtract_multiply_fusion.7 = (f32[160,1]{0,1:T(1,128)}, f32[160,1]{0,1:T(1,128)}, f32[160,1]{0,1:T(1,128)}, f32[160,1]{0,1:T(1,128)}, f32[160,1]{0,1:T(1,128)}, /*index=5*/f32[160,1]{0,1:T(1,128)}, f32[160,1]{0,1:T(1,128)}) fusion(f32[160,1]{0,1:T(1,128)S(1)} %get-tuple-element.328, f32[]{:T(128)S(6)} %rsqrt.196, f32[]{:T(128)} %get-tuple-element.208, ...), kind=kLoop, calls=%fused_computation.313 | loop fusion | flops 10080 | bytes 9740 | tf_op jit(solution)/shard_map/mul | solution.py:74
  795.8 6.5 multiply_reduce_fusion.17
  826.0 18.0 %subtract_multiply_fusion = (f32[512,1]{0,1:T(1,128)S(1)}, f32[512,1]{0,1:T(1,128)S(1)}, f32[512,1]{0,1:T(1,128)S(1)}, f32[512,1]{0,1:T(1,128)S(1)}, f32[512,1]{...) fusion(f32[512,1]{0,1:T(1,128)S(1)} %get-tuple-element.314, f32[]{:T(128)S(6)} %rsqrt.204, ...), kind=kLoop, calls=%fused_computation.222 | loop fusion | flops 32256 | bytes 30860 | tf_op jit(solution)/shard_map/mul | solution.py:74
  850.8 24.2 %all-reduce.12 = (bf16[1536,8]{0,1:T(8,128)(2,1)S(1)}, bf16[640,8]{0,1:T(8,128)(2,1)S(1)}, bf16[640,8]{0,1:T(8,128)(2,1)}) all-reduce(bf16[1536,8]{0,1:T(8,128)(2,1)S(1)} %get-tuple-element.361, bf16[640,8]{0,1:T(8,128)(2,1)} %get-tuple-element.363, bf16[640,8]{0,1:T(8,128)(2,1)} %get-tuple-element.365), channel_id=1, replica_groups=mesh['grp'=8,'blk'=4] {'grp'}, use_global_device_ids=true, to_apply=%region_175.176 | all-reduce | flops 22528 | bytes 90112 | tf_op jit(solution)/shard_map/psum | solution.py:283
  881.3 9.9 %all-gather = bf16[32768,8]{0,1:T(8,128)(2,1)} all-gather(bf16[4096,8]{0,1:T(8,128)(2,1)S(1)} %get-tuple-element.367), channel_id=2, replica_groups=mesh['grp'=8,'blk'=4] {'grp'}, dimensions={0}, use_global_device_ids=true | all-gather | bytes 589824 | tf_op jit(solution)/shard_map/all_gather | solution.py:23
  (460 shorter events, 315.0 us)
Async XLA Ops:
  7.2 564.0 %copy-start = (f32[1,4096,8]{1,2,0:T(8,128)S(1)}, f32[1,4096,8]{1,2,0:T(8,128)}, u32[]{:S(2)}) copy-start(f32[1,4096,8]{1,2,0:T(8,128)} %param.38) | copy-start | bytes 393220
  7.2 49.2 %all-gather.8.cloned.1.call-start = ((), (), s32[]{:S(2)}) async-start(), calls=%async_computation.5 | async-start | bytes 2457600 | tf_op jit(solution)/shard_map/all_gather | solution.py:117
  9.4 80.9 %all-gather.10.cloned.1.call-start = ((), (), s32[]{:S(2)}) async-start(), calls=%async_computation.6 | async-start | bytes 1310720 | tf_op jit(solution)/shard_map/all_gather | solution.py:142
  25.4 31.1 %copy-start.92 = (f32[512]{0:T(512)}, f32[512]{0:T(512)S(1)}, u32[]{:S(2)}) copy-start(f32[512]{0:T(512)S(1)} %rsqrt.166) | copy-start | bytes 6148
  26.0 34.4 %copy-start.86 = (f32[256]{0:T(256)}, f32[256]{0:T(256)S(1)}, u32[]{:S(2)}) copy-start(f32[256]{0:T(256)S(1)} %get-tuple-element.325) | copy-start | bytes 3076
  26.6 100.8 %copy-start.75 = (f32[640]{0:T(1024)}, f32[640]{0:T(1024)S(1)}, u32[]{:S(2)}) copy-start(f32[640]{0:T(1024)S(1)} %get-tuple-element.323) | copy-start | bytes 7684
  26.7 33.6 %copy-start.42 = (f32[512,128]{1,0:T(8,128)}, f32[512,128]{1,0:T(8,128)S(1)}, u32[]{:S(2)}) copy-start(f32[512,128]{1,0:T(8,128)S(1)} %broadcast_multiply_fusion.1) | copy-start | bytes 786436
  27.0 32.4 %copy-start.56 = (bf16[512,640]{1,0:T(8,128)(2,1)}, bf16[512,640]{1,0:T(8,128)(2,1)S(1)}, u32[]{:S(2)}) copy-start(bf16[512,640]{1,0:T(8,128)(2,1)S(1)} %fusion.45) | copy-start | bytes 1966084
  63.3 61.0 %all-gather.12.cloned.1.call-start = ((), (), s32[]{:S(2)}) async-start(), calls=%async_computation.7 | async-start | bytes 1638400 | tf_op jit(solution)/shard_map/all_gather | solution.py:118
  65.3 158.3 %all-gather.14.cloned.1.call-start = ((), (), s32[]{:S(2)}) async-start(), calls=%async_computation.8 | async-start | bytes 6553600 | tf_op jit(solution)/shard_map/all_gather | solution.py:119
  66.6 212.1 %all-gather.16.cloned.1.call-start = ((), (), s32[]{:S(2)}) async-start(), calls=%async_computation.9 | async-start | bytes 3276800 | tf_op jit(solution)/shard_map/all_gather | solution.py:120
  68.8 276.7 %reduce-scatter.6.cloned.1.call-start = ((), (), s32[]{:S(2)}) async-start(), calls=%async_computation.10 | async-start | bytes 1310720 | tf_op jit(solution)/shard_map/reduce_scatter | solution.py:230
  235.0 48.0 %copy-start.34 = (bf16[1,2,256,640]{3,2,1,0:T(8,128)(2,1)S(1)}, bf16[1,2,256,640]{3,2,1,0:T(8,128)(2,1)}, u32[]{:S(2)}) copy-start(bf16[1,2,256,640]{3,2,1,0:T(8,128)(2,1)} %param.21) | copy-start | bytes 1966084
  235.0 48.0 %copy-start.85 = (f32[640]{0:T(1024)S(1)}, f32[640]{0:T(1024)}, u32[]{:S(2)}) copy-start(f32[640]{0:T(1024)} %get-tuple-element.321) | copy-start | bytes 7684
  319.2 74.2 %reduce-scatter.10.cloned.1.call-start = ((), (), s32[]{:S(2)}) async-start(), calls=%async_computation.12 | async-start | bytes 1638400 | tf_op jit(solution)/shard_map/reduce_scatter | solution.py:255
  322.9 109.1 %reduce-scatter.14.cloned.1.call-start = ((), (), s32[]{:S(2)}) async-start(), calls=%async_computation.14 | async-start | bytes 3276800 | tf_op jit(solution)/shard_map/reduce_scatter | solution.py:261
  327.5 148.7 %reduce-scatter.8.cloned.1.call-start = ((), (), s32[]{:S(2)}) async-start(), calls=%async_computation.11 | async-start | bytes 2457600 | tf_op jit(solution)/shard_map/reduce_scatter | solution.py:252
  363.2 208.0 %reduce-scatter.12.cloned.1.call-start = ((), (), s32[]{:S(2)}) async-start(), calls=%async_computation.13 | async-start | bytes 6553600 | tf_op jit(solution)/shard_map/reduce_scatter | solution.py:258
  393.4 40.9 %copy-start.90 = (f32[1,640,8]{1,2,0:T(8,128)S(1)}, f32[1,640,8]{1,2,0:T(8,128)}, u32[]{:S(2)}) copy-start(f32[1,640,8]{1,2,0:T(8,128)} %param.39) | copy-start | bytes 61444
  396.9 79.2 %copy-start.79 = (f32[1,1536,8]{1,2,0:T(8,128)S(1)}, f32[1,1536,8]{1,2,0:T(8,128)}, u32[]{:S(2)}) copy-start(f32[1,1536,8]{1,2,0:T(8,128)} %param.36) | copy-start | bytes 147460
  434.3 136.9 %copy-start.6 = (f32[1,160,4096]{2,1,0:T(8,128)S(1)}, f32[1,160,4096]{2,1,0:T(8,128)}, u32[]{:S(2)}) copy-start(f32[1,160,4096]{2,1,0:T(8,128)} %param.34) | copy-start | bytes 7864324
  844.0 66.1 %copy-start.65 = (f32[160,8]{0,1:T(8,128)}, f32[160,8]{0,1:T(8,128)S(1)}, u32[]{:S(2)}) copy-start(f32[160,8]{0,1:T(8,128)S(1)} %stack.23) | copy-start | bytes 15364
  844.8 67.4 %copy-start.66 = (f32[256,8]{0,1:T(8,128)}, f32[256,8]{0,1:T(8,128)S(1)}, u32[]{:S(2)}) copy-start(f32[256,8]{0,1:T(8,128)S(1)} %stack.24) | copy-start | bytes 24580
  844.8 73.0 %copy-start.64 = (f32[512,8]{0,1:T(8,128)}, f32[512,8]{0,1:T(8,128)S(1)}, u32[]{:S(2)}) copy-start(f32[512,8]{0,1:T(8,128)S(1)} %stack.26) | copy-start | bytes 49156
  (103 other events, 473.0 us)
Sparse Core Ops, SparseCore 0:
  10.2 46.2 all-gather.7
  63.5 26.7 all-gather.9
  92.4 31.8 all-gather.11
  126.4 97.1 all-gather.13
  225.5 53.0 all-gather.15
  319.4 26.0 reduce-scatter.5
  348.3 29.8 reduce-scatter.9
  381.1 50.8 reduce-scatter.13
  434.9 41.1 reduce-scatter.7
  478.3 92.8 reduce-scatter.11
